TPU v7x, 512 devices: a whole 4x4x16 slice. The times are simulated.
512 devices in a mesh: clips: 32 (over y, x, core), slab: 16 (over z).
Axes of the slice: x: 4, y: 4, z: 16, core: 2. Of those that a mesh axis runs over, the one named last changes fastest.
Arguments:
- video: bfloat16 [64, 6, 16, 16, 256], P('clips', None, 'slab'), may hold values from -6 to 6
- clip_blocks: int32 [64], replicated, may hold values from 1 to 3, 128 in all
- deal_order: int32 [32], replicated, may hold values from 0 to 31, each once
- kernel: bfloat16 [256, 3456], P('clips', 'slab'), may hold values from -0.078125 to 0.078125
- gain: float32 [128], replicated, may hold values from 0.25 to 1.75
- bias: float32 [128], replicated, may hold values from -3 to 3
- cotangent: bfloat16 [128, 2, 16, 16, 128], P('clips', None, 'slab'), may hold values from -6 to 6
Outputs:
- activations: bfloat16 [128, 2, 16, 16, 128], P('clips', None, 'slab')
- video_grad: bfloat16 [64, 6, 16, 16, 256], P('clips', None, 'slab')
- kernel_grad: float32 [256, 3456], P('clips', 'slab')
- gain_grad: float32 [128], replicated
- bias_grad: float32 [128], replicated
Inputs may be any that keep to these rules, and one draw needn't show every extreme that they name: `clip_blocks`: the blocks of all clips add up to 4 times the number of devices along clips, so every device receives exactly 4 blocks; some clip has 3 blocks. `deal_order`: a permutation of the devices along clips.
All inputs are finite; a program needn't handle non-finite values.
Results may differ from a plain program's by a relative error of at most 0.0049.
Values may be sent and summed in bfloat16 or wider, within the bound.
A program may use at most 64 MiB of HBM per device.

v0:
```python
import jax
import jax.numpy as jnp
from jax import lax
from jax.sharding import PartitionSpec as P

GROUPS = 16
TAPS = 27
FB = 2
BMAX = 3


def extended(array, sides, width):
    for axis, dim in sides:
        size, length = (lax.axis_size(axis), array.shape[dim])
        up = [(i, (i + 1) % size) for i in range(size - 1)]
        down = [(j, i) for i, j in up]
        last = lax.slice_in_dim(array, length - width, length, axis=dim)
        initial = lax.slice_in_dim(array, 0, width, axis=dim)
        before = lax.ppermute(last, axis, up)
        after = lax.ppermute(initial, axis, down)
        array = jnp.concatenate([before, array, after], axis=dim)
    return array


def body(video, clip_blocks, deal_order, kernel, gain, bias, cotangent):
    clip_devs = lax.axis_size("clips")
    slab_devs = lax.axis_size("slab")
    own_index = lax.axis_index("clips")
    held_clips, frame_count, row_count, column_count, in_channels = video.shape
    slot_count = cotangent.shape[0]
    out_channels = gain.shape[0]
    all_clips = clip_blocks.shape[0]
    per_group = out_channels // GROUPS
    capacity = -(-(held_clips * BMAX) // clip_devs)
    block_ends = jnp.cumsum(clip_blocks)
    block_starts = block_ends - clip_blocks
    device_ids = jnp.arange(clip_devs, dtype=jnp.int32)
    deal_slot = jnp.sum(
        jnp.where(deal_order[:, None] == device_ids[None, :], device_ids[:, None], 0), axis=0
    )
    first_clip = own_index * held_clips
    own_start = block_starts[first_clip]
    own_end = block_ends[first_clip + held_clips - 1]
    dest_rank = jnp.repeat(device_ids, capacity)
    turn_index = jnp.tile(jnp.arange(capacity, dtype=jnp.int32), clip_devs)
    slot_blocks = jnp.arange(slot_count, dtype=jnp.int32) * clip_devs + deal_slot[own_index]

    def clip_index(block_id):
        return jnp.sum((block_ends <= block_id[..., None]).astype(jnp.int32), axis=-1)

    full_kernel = lax.all_gather(kernel, "slab", axis=1, tiled=True)
    full_kernel = lax.all_gather(full_kernel, "clips", axis=0, tiled=True)
    kernel_taps = full_kernel.reshape(in_channels, out_channels, TAPS).transpose(2, 0, 1)

    def group_sums(values):
        return jnp.sum(values.reshape(values.shape[:4] + (GROUPS, per_group)), axis=(1, 2, 3, 5))

    def spread(stat):
        return stat[:, None, None, None, :, None]

    cells_clip = FB * row_count * slab_devs * column_count * per_group
    context_video = jnp.pad(video, ((0, 0), (2, 0), (0, 0), (0, 0), (0, 0)))
    highest = lax.Precision.HIGHEST
    first_block = own_start + jnp.mod(deal_slot[dest_rank] - own_start, clip_devs)
    block_id = first_block + turn_index * clip_devs
    is_live = block_id < own_end
    clip_global = jnp.minimum(clip_index(block_id), all_clips - 1)
    clip_local = jnp.clip(clip_global - first_clip, 0, held_clips - 1)
    block_local = jnp.clip(block_id - block_starts[clip_global], 0, BMAX - 1)
    window = FB + 2

    def window_of(clip_pick, block_pick):
        begin = (clip_pick, block_pick * FB, 0, 0, 0)
        sizes = (1, window, row_count, column_count, context_video.shape[-1])
        return lax.dynamic_slice(context_video, begin, sizes)[0]

    pieces = jax.vmap(window_of)(clip_local, block_local)
    pieces = jnp.where(
        is_live[:, None, None, None, None], pieces, jnp.zeros((), context_video.dtype)
    )
    sent = pieces.reshape((clip_devs, capacity) + pieces.shape[1:])
    received = lax.all_to_all(sent, "clips", split_axis=0, concat_axis=0, tiled=True)
    clip_global = clip_index(slot_blocks)
    source_rank = clip_global // held_clips
    turn_of = (slot_blocks - block_starts[source_rank * held_clips]) // clip_devs
    flat_rows = received.reshape((clip_devs * capacity,) + received.shape[2:])
    input_slots = flat_rows[source_rank * capacity + turn_of]
    rimmed = extended(input_slots, (("slab", 2),), 1)
    padded = jnp.pad(rimmed, ((0, 0), (0, 0), (0, 0), (1, 1), (0, 0)))
    forward_outputs = input_slots.shape[1] - 2
    totals = jnp.zeros(
        (input_slots.shape[0] * forward_outputs * row_count * column_count, out_channels),
        jnp.float32,
    )
    for forward_step_a in range(3):
        for forward_step_b in range(3):
            for forward_step_c in range(3):
                tap_rows = padded[
                    :,
                    forward_step_a : forward_step_a + forward_outputs,
                    forward_step_b : forward_step_b + row_count,
                    forward_step_c : forward_step_c + column_count,
                    :,
                ].reshape(-1, in_channels)
                totals = totals + jnp.dot(
                    tap_rows,
                    kernel_taps[(forward_step_a * 3 + forward_step_b) * 3 + forward_step_c],
                    preferred_element_type=jnp.float32,
                )
    conv_out = totals.reshape(
        input_slots.shape[0], forward_outputs, row_count, column_count, out_channels
    )
    slot_clip = clip_index(slot_blocks)
    chooser = (slot_clip[:, None] == jnp.arange(all_clips, dtype=jnp.int32)[None, :]).astype(
        jnp.float32
    )
    table_first = jnp.dot(chooser.T, group_sums(conv_out), precision=highest)
    table_second = jnp.dot(chooser.T, group_sums(conv_out * conv_out), precision=highest)
    table_first, table_second = lax.psum((table_first, table_second), ("clips", "slab"))
    counts = (clip_blocks * cells_clip).astype(jnp.float32)
    group_mean = table_first / counts[:, None]
    group_var = table_second / counts[:, None] - group_mean * group_mean
    clip_mean = group_mean
    clip_inv = lax.rsqrt(group_var + 1e-05)
    group_mean = jnp.dot(chooser, clip_mean, precision=highest)
    inv_std = jnp.dot(chooser, clip_inv, precision=highest)
    grouped = conv_out.reshape(conv_out.shape[:4] + (GROUPS, per_group))
    normed = ((grouped - spread(group_mean)) * spread(inv_std)).reshape(conv_out.shape)
    affine = normed * gain + bias
    activations = jax.nn.silu(affine).astype(jnp.bfloat16)
    sigmoid = jax.nn.sigmoid(affine)
    grad_affine = cotangent.astype(jnp.float32) * sigmoid * (1.0 + affine * (1.0 - sigmoid))
    gain_part = jnp.sum(grad_affine * normed, axis=(0, 1, 2, 3))
    bias_part = jnp.sum(grad_affine, axis=(0, 1, 2, 3))
    grad_normed, gain_part, bias_part = (grad_affine * gain, gain_part, bias_part)
    sum_grad = jnp.dot(chooser.T, group_sums(grad_normed), precision=highest)
    sum_cross = jnp.dot(chooser.T, group_sums(grad_normed * normed), precision=highest)
    sum_grad, sum_cross, gain_grad, bias_grad = lax.psum(
        (sum_grad, sum_cross, gain_part, bias_part), ("clips", "slab")
    )
    mean_grad = jnp.dot(chooser, sum_grad / counts[:, None], precision=highest)
    mean_cross = jnp.dot(chooser, sum_cross / counts[:, None], precision=highest)
    grouped = grad_normed.reshape(grad_normed.shape[:4] + (GROUPS, per_group))
    normed_groups = normed.reshape(grouped.shape)
    result = spread(inv_std) * (grouped - spread(mean_grad) - normed_groups * spread(mean_cross))
    grad_conv = result.reshape(grad_normed.shape).astype(jnp.bfloat16)
    range_start = block_starts[dest_rank * held_clips]
    range_end = block_ends[dest_rank * held_clips + held_clips - 1]
    first_block = range_start + jnp.mod(deal_slot[own_index] - range_start, clip_devs)
    block_id = first_block + turn_index * clip_devs
    is_live = block_id < range_end
    slot_index = jnp.clip(block_id // clip_devs, 0, slot_count - 1)
    pieces = jnp.where(
        is_live[:, None, None, None, None], grad_conv[slot_index], jnp.zeros((), grad_conv.dtype)
    )
    returned = lax.all_to_all(
        pieces.reshape((clip_devs, capacity) + pieces.shape[1:]),
        "clips",
        split_axis=0,
        concat_axis=0,
        tiled=True,
    )
    clip_global = first_clip + jnp.arange(held_clips, dtype=jnp.int32)[:, None]
    block_range = jnp.arange(BMAX, dtype=jnp.int32)[None, :]
    block_id = block_starts[clip_global] + block_range
    is_live = block_range < clip_blocks[clip_global]
    source_rank = deal_order[jnp.mod(block_id, clip_devs)]
    turn_of = (block_id - own_start) // clip_devs
    row_index = jnp.where(is_live, source_rank * capacity + turn_of, 0)
    flat_rows = returned.reshape((clip_devs * capacity,) + returned.shape[2:])
    pieces = jnp.where(
        is_live[:, :, None, None, None, None], flat_rows[row_index], jnp.zeros((), returned.dtype)
    )
    grad_clip = pieces.reshape((held_clips, frame_count) + pieces.shape[3:])
    rimmed_grad = extended(grad_clip, (("slab", 2),), 1)
    grad_padded = jnp.pad(rimmed_grad, ((0, 0), (0, 2), (0, 0), (1, 1), (0, 0)))
    totals = jnp.zeros(
        (held_clips * frame_count * row_count * column_count, in_channels), jnp.float32
    )
    for step_a in range(3):
        for step_b in range(3):
            for step_c in range(3):
                moved = grad_padded[
                    :,
                    2 - step_a : 2 - step_a + frame_count,
                    2 - step_b : 2 - step_b + row_count,
                    2 - step_c : 2 - step_c + column_count,
                    :,
                ].reshape(-1, out_channels)
                totals = totals + lax.dot_general(
                    moved,
                    kernel_taps[(step_a * 3 + step_b) * 3 + step_c],
                    (((1,), (1,)), ((), ())),
                    preferred_element_type=jnp.float32,
                )
    video_grad = totals.reshape(video.shape).astype(jnp.bfloat16)
    outputs = grad_conv.shape[1]
    grad_flat = grad_conv.reshape(-1, out_channels)
    take_count = in_channels // clip_devs * lax.axis_size("clips")
    tap_parts = []
    for step_a in range(3):
        for step_b in range(3):
            for step_c in range(3):
                tap_rows = padded[
                    :,
                    step_a : step_a + outputs,
                    step_b : step_b + row_count,
                    step_c : step_c + column_count,
                    :,
                ].reshape(-1, take_count)
                tap_parts.append(
                    lax.dot_general(
                        tap_rows,
                        grad_flat,
                        (((0,), (0,)), ((), ())),
                        preferred_element_type=jnp.float32,
                    )
                )
    partial_grad = lax.psum_scatter(
        jnp.stack(tap_parts, axis=2).reshape(take_count, out_channels * TAPS),
        "clips",
        scatter_dimension=0,
        tiled=True,
    )
    kernel_grad = lax.psum_scatter(partial_grad, "slab", scatter_dimension=1, tiled=True)
    return (activations, video_grad, kernel_grad, gain_grad, bias_grad)


def solution(mesh):
    return jax.shard_map(
        body,
        mesh=mesh,
        in_specs=(
            P("clips", None, "slab", None, None),
            P(),
            P(),
            P("clips", "slab"),
            P(),
            P(),
            P("clips", None, "slab", None, None),
        ),
        out_specs=(
            P("clips", None, "slab", None, None),
            P("clips", None, "slab", None, None),
            P("clips", "slab"),
            P(),
            P(),
        ),
        check_vma=False,
    )
```

profile of v0, /device:TPU:1, one launch (start us, length us, event | category | flops | bytes accessed | tf_op | source)
XLA Modules:
  0.0 633.4 jit_solution(1696978957917538280)
XLA Ops:
  9.0 1.2 multiply_convert_fusion.2
  12.8 1.3 broadcast_compare_fusion
  16.4 1.1 fusion.36
  17.6 10.4 %all-to-all-start = ((bf16[32,1,4,1,16,256]{5,4,2,3,1,0:T(8,128)(2,1)}), bf16[32,1,4,1,16,256]{5,4,2,3,1,0:T(8,128)(2,1)S(1)}, u32[]{:S(2)}, u32[]{:S(2)}) async-start(bf16[32,1,4,1,16,256]{5,4,2,3,1,0:T(8,128)(2,1)} %fusion.36), calls=%async_computation | async-start | bytes 2097152 | tf_op jit(solution)/shard_map/all_to_all | solution.py:82
  28.0 27.6 %all-gather = bf16[16,216,8]{1,2,0:T(8,128)(2,1)S(1)} all-gather(bf16[1,216,8]{1,2,0:T(8,128)(2,1)S(1)} %bitcast.755), channel_id=1, replica_groups=mesh['clips'=32,'slab'=16] {'slab'}, dimensions={0}, use_global_device_ids=true | all-gather | bytes 58752 | tf_op jit(solution)/shard_map/all_gather | solution.py:51
  63.8 1.3 dynamic-slice.1
  68.3 1.3 collective-permute-start.1
  69.6 4.0 collective-permute-start
  74.3 1.2 collective-permute-done
  78.2 39.2 %all-gather.3.cloned.1.call-done = bf16[256,3456]{1,0:T(8,128)(2,1)} async-done(((bf16[8,3456]{1,0:T(8,128)(2,1)}), bf16[256,3456]{1,0:T(8,128)(2,1)}) %all-gather.3.cloned.1.call-update) | async-done | bytes 1769488 | tf_op jit(solution)/shard_map/all_gather | solution.py:52
  117.4 3.9 copy.95
  121.3 2.6 reshape.1229
  123.9 3.5 fusion.224
  127.3 1.8 fusion.225
  129.2 1.1 copy.122
  130.3 1.0 copy.116
  131.3 1.0 copy.113
  135.7 1.0 copy.99
  136.8 1.0 copy.100
  137.8 1.0 copy.101
  172.9 103.8 %all-reduce.6 = (f32[64,16]{0,1:T(8,128)S(1)}, f32[64,16]{0,1:T(8,128)S(1)}) all-reduce(f32[64,16]{0,1:T(8,128)S(1)} %fusion.160, f32[64,16]{0,1:T(8,128)S(1)} %fusion.161), channel_id=1, replica_groups=mesh['clips'=32,'slab'=16] {'clips','slab'}, use_global_device_ids=true, to_apply=%region_7.8 | all-reduce | flops 2048 | bytes 16384 | tf_op jit(solution)/shard_map/psum | solution.py:119
  279.0 100.7 %all-reduce.5 = (f32[64,16]{0,1:T(8,128)S(1)}, f32[64,16]{0,1:T(8,128)S(1)}, f32[128]{0:T(128)}, f32[128]{0:T(128)}) all-reduce(f32[64,16]{0,1:T(8,128)S(1)} %fusion.158, f32[64,16]{0,1:T(8,128)S(1)} %fusion.159, f32[128]{0:T(128)S(1)} %get-tuple-element.25, ...), channel_id=1, replica_groups=mesh['clips'=32,'slab'=16] {'clips','slab'}, use_global_device_ids=true, to_apply=%region_13.14 | all-reduce | flops 2304 | bytes 18432 | tf_op jit(solution)/shard_map/psum | solution.py:138
  382.7 4.8 all-to-all-start.1
  410.2 6.0 copy.126
  416.2 4.9 reshape.1311
  421.8 1.3 collective-permute-start.3
  423.1 4.0 collective-permute-start.2
  427.2 1.1 collective-permute-done.2
  433.3 125.9 %all-reduce.9.cloned.1.call-done = f32[256,3456]{0,1:T(8,128)} async-done(((f32[256,3456]{0,1:T(8,128)}), f32[256,3456]{0,1:T(8,128)}) %all-reduce.9.cloned.1.call-update) | async-done | bytes 3538960
  559.2 3.2 constant_dynamic-slice_fusion
  563.3 62.0 %reduce-scatter.5.cloned.1.call-done = f32[8,216]{0,1:T(8,128)} async-done(((f32[8,3456]{0,1:T(8,128)}), f32[8,216]{0,1:T(8,128)}) %reduce-scatter.5.cloned.1.call-update) | async-done | bytes 6928
  625.3 1.6 copy.128
  (247 shorter events, 92.2 us)
Async XLA Ops:
  14.2 13.8 %copy-start.15 = (bf16[8,216]{1,0:T(8,128)(2,1)S(1)}, bf16[8,216]{1,0:T(8,128)(2,1)}, u32[]{:S(2)}) copy-start(bf16[8,216]{1,0:T(8,128)(2,1)} %param.10) | copy-start | bytes 10372
  15.7 41.5 %copy-start.1 = (s32[64]{0:T(128)S(1)}, s32[64]{0:T(128)}, u32[]{:S(2)}) copy-start(s32[64]{0:T(128)} %param.8) | copy-start | bytes 772
  15.7 42.9 %copy-start = (s32[32]{0:T(128)S(1)}, s32[32]{0:T(128)}, u32[]{:S(2)}) copy-start(s32[32]{0:T(128)} %param.9) | copy-start | bytes 388
  17.6 50.2 %all-to-all-start = ((bf16[32,1,4,1,16,256]{5,4,2,3,1,0:T(8,128)(2,1)}), bf16[32,1,4,1,16,256]{5,4,2,3,1,0:T(8,128)(2,1)S(1)}, u32[]{:S(2)}, u32[]{:S(2)}) async-start(bf16[32,1,4,1,16,256]{5,4,2,3,1,0:T(8,128)(2,1)} %fusion.36), calls=%async_computation | async-start | bytes 2097152 | tf_op jit(solution)/shard_map/all_to_all | solution.py:82
  28.0 89.4 %all-gather.3.cloned.1.call-start = ((), (), s32[]{:S(2)}) async-start(), calls=%async_computation.3 | async-start | bytes 1824768 | tf_op jit(solution)/shard_map/all_gather | solution.py:52
  60.1 8.2 %copy-start.20 = (s32[4]{0:T(128)}, s32[4]{0:T(128)S(1)}, u32[]{:S(2)}) copy-start(s32[4]{0:T(128)S(1)} %convert_reduce_fusion.1) | copy-start | bytes 52
  68.3 6.0 collective-permute-start.1
  69.6 5.9 collective-permute-start
  129.1 17.0 %copy-start.8 = (bf16[1,256,128]{1,0,2:T(2,128)(2,1)S(1)}, bf16[1,256,128]{1,0,2:T(2,128)(2,1)}, u32[]{:S(2)}) copy-start(bf16[1,256,128]{1,0,2:T(2,128)(2,1)} %get-tuple-element.49) | copy-start | bytes 196612
  129.1 18.2 %copy-start.7 = (bf16[1,256,128]{1,0,2:T(2,128)(2,1)S(1)}, bf16[1,256,128]{1,0,2:T(2,128)(2,1)}, u32[]{:S(2)}) copy-start(bf16[1,256,128]{1,0,2:T(2,128)(2,1)} %get-tuple-element.46) | copy-start | bytes 196612
  129.1 18.4 %copy-start.6 = (bf16[1,256,128]{1,0,2:T(2,128)(2,1)S(1)}, bf16[1,256,128]{1,0,2:T(2,128)(2,1)}, u32[]{:S(2)}) copy-start(bf16[1,256,128]{1,0,2:T(2,128)(2,1)} %get-tuple-element.45) | copy-start | bytes 196612
  129.1 18.5 %copy-start.5 = (bf16[1,256,128]{1,0,2:T(2,128)(2,1)S(1)}, bf16[1,256,128]{1,0,2:T(2,128)(2,1)}, u32[]{:S(2)}) copy-start(bf16[1,256,128]{1,0,2:T(2,128)(2,1)} %get-tuple-element.43) | copy-start | bytes 196612
  129.1 18.6 %copy-start.4 = (bf16[1,256,128]{1,0,2:T(2,128)(2,1)S(1)}, bf16[1,256,128]{1,0,2:T(2,128)(2,1)}, u32[]{:S(2)}) copy-start(bf16[1,256,128]{1,0,2:T(2,128)(2,1)} %get-tuple-element.42) | copy-start | bytes 196612
  129.1 18.8 %copy-start.3 = (bf16[1,256,128]{1,0,2:T(2,128)(2,1)S(1)}, bf16[1,256,128]{1,0,2:T(2,128)(2,1)}, u32[]{:S(2)}) copy-start(bf16[1,256,128]{1,0,2:T(2,128)(2,1)} %get-tuple-element.41) | copy-start | bytes 196612
  129.1 18.9 %copy-start.2 = (bf16[1,256,128]{1,0,2:T(2,128)(2,1)S(1)}, bf16[1,256,128]{1,0,2:T(2,128)(2,1)}, u32[]{:S(2)}) copy-start(bf16[1,256,128]{1,0,2:T(2,128)(2,1)} %get-tuple-element.40) | copy-start | bytes 196612
  129.1 23.2 %copy-start.9 = (bf16[4,2,1,16,256]{4,3,1,0,2:T(8,128)(2,1)S(1)}, bf16[4,2,1,16,256]{4,3,1,0,2:T(8,128)(2,1)}, u32[]{:S(2)}) copy-start(bf16[4,2,1,16,256]{4,3,1,0,2:T(8,128)(2,1)} %get-tuple-element.76) | copy-start | bytes 196612
  147.4 21.2 %copy-start.12 = (bf16[4,2,1,16,256]{4,3,1,0,2:T(8,128)(2,1)S(1)}, bf16[4,2,1,16,256]{4,3,1,0,2:T(8,128)(2,1)}, u32[]{:S(2)}) copy-start(bf16[4,2,1,16,256]{4,3,1,0,2:T(8,128)(2,1)} %get-tuple-element.67) | copy-start | bytes 196612
  147.8 22.0 %copy-start.11 = (bf16[4,2,1,16,256]{4,3,1,0,2:T(8,128)(2,1)S(1)}, bf16[4,2,1,16,256]{4,3,1,0,2:T(8,128)(2,1)}, u32[]{:S(2)}) copy-start(bf16[4,2,1,16,256]{4,3,1,0,2:T(8,128)(2,1)} %get-tuple-element.66) | copy-start | bytes 196612
  147.9 22.0 %copy-start.10 = (bf16[4,2,1,16,256]{4,3,1,0,2:T(8,128)(2,1)S(1)}, bf16[4,2,1,16,256]{4,3,1,0,2:T(8,128)(2,1)}, u32[]{:S(2)}) copy-start(bf16[4,2,1,16,256]{4,3,1,0,2:T(8,128)(2,1)} %get-tuple-element.65) | copy-start | bytes 196612
  148.2 21.9 %copy-start.13 = (bf16[4,2,1,16,256]{4,3,1,0,2:T(8,128)(2,1)S(1)}, bf16[4,2,1,16,256]{4,3,1,0,2:T(8,128)(2,1)}, u32[]{:S(2)}) copy-start(bf16[4,2,1,16,256]{4,3,1,0,2:T(8,128)(2,1)} %get-tuple-element.107) | copy-start | bytes 196612
  153.6 17.8 %copy-start.21 = (s32[4]{0:T(128)S(1)}, s32[4]{0:T(128)}, u32[]{:S(2)}) copy-start(s32[4]{0:T(128)} %copy-done.20) | copy-start | bytes 52
  158.6 118.1 %copy-start.19 = (f32[64]{0:T(128)S(1)}, f32[64]{0:T(128)}, u32[]{:S(2)}) copy-start(f32[64]{0:T(128)} %get-tuple-element.117) | copy-start | bytes 772
  159.6 117.8 %copy-start.14 = (bf16[4,2,1,16,128]{4,3,2,1,0:T(8,128)(2,1)S(1)}, bf16[4,2,1,16,128]{4,3,2,1,0:T(8,128)(2,1)}, u32[]{:S(2)}) copy-start(bf16[4,2,1,16,128]{4,3,2,1,0:T(8,128)(2,1)} %param.13) | copy-start | bytes 98308
  159.6 117.8 %copy-start.16 = (f32[128]{0:T(128)S(1)}, f32[128]{0:T(128)}, u32[]{:S(2)}) copy-start(f32[128]{0:T(128)} %param.11) | copy-start | bytes 1540
  159.6 117.8 %copy-start.17 = (f32[128]{0:T(128)S(1)}, f32[128]{0:T(128)}, u32[]{:S(2)}) copy-start(f32[128]{0:T(128)} %param.12) | copy-start | bytes 1540
  382.7 38.4 %all-to-all-start.1 = ((bf16[32,1,2,1,16,128]{5,4,2,3,1,0:T(8,128)(2,1)}), bf16[32,1,2,1,16,128]{5,4,2,3,1,0:T(8,128)(2,1)S(1)}, u32[]{:S(2)}, u32[]{:S(2)}) async-start(bf16[32,1,2,1,16,128]{5,4,2,3,1,0:T(8,128)(2,1)} %bitcast_select_fusion.1), calls=%async_computation.1 | async-start | bytes 524288 | tf_op jit(solution)/shard_map/all_to_all | solution.py:156
  387.5 171.7 %all-reduce.9.cloned.1.call-start = ((), (), s32[]{:S(2)}) async-start(), calls=%async_computation.4 | async-start | bytes 7077888
  421.1 0.7 copy-start.18
  421.1 204.2 %reduce-scatter.5.cloned.1.call-start = ((), (), s32[]{:S(2)}) async-start(), calls=%async_computation.5 | async-start | bytes 1880064
  421.8 5.4 collective-permute-start.3
  423.1 5.2 collective-permute-start.2
Sparse Core Ops, SparseCore 0:
  56.6 60.7 all-gather.2
  421.2 137.9 all-reduce.8
  562.6 62.6 reduce-scatter.4
where the time goes:
time: 645 us; the launch traced here: 633 us
  blocking collectives  232 us (36%)
  waiting for transfers between devices  229 us (36%)
  local copies, waits for them, and re-layouts  66.3 us (10%)
  matrix products  52.1 us (8%)
  starting transfers between devices  25.9 us (4%)
  between operations  15.4 us (2%)
  other arithmetic  12.1 us (2%)
    unnamed x5, waiting for transfers between devices  188 us
    psum x1, blocking collectives, body(): lax.psum((table_first, table_second), ('clips', 'slab'))  104 us
    psum x1, blocking collectives, body(): lax.psum((sum_grad, sum_cross, gain_part, bias_part), ('clips', 'slab'))  101 us
    all_gather x1, waiting for transfers between devices, body(): full_kernel = lax.all_gather(full_kernel, 'clips', axis=0, tiled=True)  39.2 us
    all_gather x1, blocking collectives, body(): full_kernel = lax.all_gather(kernel, 'slab', axis=1, tiled=True)  27.6 us
    slice x29, local copies, waits for them, and re-layouts, body(): kernel_taps[(forward_step_a * 3 + forward_step_b) * 3 + forward_step_c]  24.2 us
    dot_general x27, matrix products, body(): lax.dot_general(tap_rows, grad_flat, (((0,), (0,)), ((), ())), preferred_...  23.5 us
    dot_general x27, matrix products, body(): jnp.dot(tap_rows, kernel_taps[(forward_step_a * 3 + forward_step_b) * 3 +...  21.6 us
  transfers between devices with their start and end apart: 9, of which 5 were waited for; matrix products, arithmetic and copies ran while one was open for 9% of the time, Pallas kernels for 0%

commit v1 on v0

v1 whole, which is shorter than its diff:
```python
import functools

import jax
import jax.numpy as jnp
from jax import lax
from jax.experimental import pallas as pl
from jax.experimental.pallas import tpu as pltpu
from jax.sharding import PartitionSpec as P

GROUPS = 16
TAPS = 27
FB = 2
BMAX = 3
MESH = pl.DeviceIdType.MESH


def extended(array, axis, dim):
    size, length = (lax.axis_size(axis), array.shape[dim])
    up = [(i, i + 1) for i in range(size - 1)]
    down = [(j, i) for i, j in up]
    before = lax.ppermute(lax.slice_in_dim(array, length - 1, length, axis=dim), axis, up)
    after = lax.ppermute(lax.slice_in_dim(array, 0, 1, axis=dim), axis, down)
    return jnp.concatenate([before, array, after], axis=dim)


def greet(axis, n, me):
    barrier = pltpu.get_barrier_semaphore()

    def signal(k, carry):
        pl.semaphore_signal(
            barrier, inc=1, device_id={axis: lax.rem(me + k, n)}, device_id_type=MESH
        )
        return carry

    lax.fori_loop(1, n, signal, 0)
    pl.semaphore_wait(barrier, n - 1)


def remote(axis, peer, src, dst, sends, recvs, k):
    return pltpu.make_async_remote_copy(
        src_ref=src,
        dst_ref=dst,
        send_sem=sends.at[k],
        recv_sem=recvs.at[k],
        device_id={axis: peer},
        device_id_type=MESH,
    )


def gather_kernel(axis, n, inner, x_ref, out_ref, sends, recvs, own):
    me = lax.axis_index(axis)
    greet(axis, n, me)
    place = out_ref.at[:, me] if inner else out_ref.at[me]

    def copy(k):
        return remote(axis, lax.rem(me + k, n), x_ref, place, sends, recvs, k)

    def start(k, carry):
        copy(k).start()
        return carry

    def wait(k, carry):
        copy(k).wait()
        return carry

    lax.fori_loop(1, n, start, 0)
    local = pltpu.make_async_copy(x_ref, place, own)
    local.start()
    local.wait()
    lax.fori_loop(1, n, wait, 0)


def gather(x, axis, inner, collective_id):
    n = lax.axis_size(axis)
    shape = (x.shape[0], n) + x.shape[1:] if inner else (n,) + x.shape
    return pl.pallas_call(
        functools.partial(gather_kernel, axis, n, inner),
        out_shape=jax.ShapeDtypeStruct(shape, x.dtype),
        in_specs=[pl.BlockSpec(memory_space=pltpu.VMEM)],
        out_specs=pl.BlockSpec(memory_space=pltpu.VMEM),
        scratch_shapes=[
            pltpu.SemaphoreType.DMA((n,)),
            pltpu.SemaphoreType.DMA((n,)),
            pltpu.SemaphoreType.DMA,
        ],
        compiler_params=pltpu.CompilerParams(collective_id=collective_id, has_side_effects=True),
    )(x)


def reduce_kernel(axis, n, parts, *refs):
    count = len(parts)
    ins, outs = refs[:count], refs[count : 2 * count]
    held, sends, recvs = (refs[2 * count + p * count : 2 * count + (p + 1) * count] for p in range(3))
    own = refs[5 * count]
    me = lax.axis_index(axis)
    greet(axis, n, me)

    def block(p, which):
        if parts[p] is None:
            return ins[p]
        return ins[p].at[which] if parts[p] == 0 else ins[p].at[:, which]

    def copy(p, k):
        peer = lax.rem(me + k, n)
        return remote(axis, peer, block(p, peer), held[p].at[me], sends[p], recvs[p], k)

    def start(k, carry):
        for p in range(count):
            copy(p, k).start()
        return carry

    def wait(k, carry):
        for p in range(count):
            copy(p, k).wait()
        return carry

    lax.fori_loop(1, n, start, 0)
    for p in range(count):
        local = pltpu.make_async_copy(block(p, me), held[p].at[me], own)
        local.start()
        local.wait()
    lax.fori_loop(1, n, wait, 0)
    for p in range(count):
        outs[p][...] = jnp.zeros(outs[p].shape, jnp.float32)

        def add(k, carry):
            outs[p][...] += held[p][k].astype(jnp.float32)
            return carry

        lax.fori_loop(0, n, add, 0)


def reduce(xs, parts, axis, collective_id):
    n = lax.axis_size(axis)
    shapes = []
    for x, part in zip(xs, parts):
        shape = list(x.shape)
        if part is not None:
            del shape[part]
        shapes.append(tuple(shape))
    vmem = pl.BlockSpec(memory_space=pltpu.VMEM)
    count = len(xs)
    return pl.pallas_call(
        functools.partial(reduce_kernel, axis, n, parts),
        out_shape=[jax.ShapeDtypeStruct(shape, jnp.float32) for shape in shapes],
        in_specs=[vmem] * count,
        out_specs=[vmem] * count,
        scratch_shapes=[pltpu.VMEM((n,) + shape, x.dtype) for x, shape in zip(xs, shapes)]
        + [pltpu.SemaphoreType.DMA((n,))] * (2 * count)
        + [pltpu.SemaphoreType.DMA],
        compiler_params=pltpu.CompilerParams(collective_id=collective_id, has_side_effects=True),
    )(*xs)


def picked(mask, array):
    mask = mask.reshape(mask.shape + (1,) * (array.ndim - 1))
    return jnp.sum(jnp.where(mask, array[None], jnp.zeros((), array.dtype)), axis=1)


def nine(padded, columns, flip):
    order = (2, 1, 0) if flip else (0, 1, 2)
    return jnp.concatenate(
        [padded[:, :, b, e : e + columns, :] for b in order for e in order], axis=-1
    )


def body(video, clip_blocks, deal_order, kernel, gain, bias, cotangent):
    clip_devs = lax.axis_size("clips")
    slab_devs = lax.axis_size("slab")
    own_index = lax.axis_index("clips")
    held, frames, row_count, columns, in_channels = video.shape
    slot_count = cotangent.shape[0]
    out_channels = gain.shape[0]
    per_group = out_channels // GROUPS
    capacity = -(-(held * BMAX) // clip_devs)
    highest = lax.Precision.HIGHEST
    block_ends = jnp.cumsum(clip_blocks)
    block_starts = block_ends - clip_blocks
    device_ids = jnp.arange(clip_devs, dtype=jnp.int32)
    deal_slot = jnp.sum(
        jnp.where(deal_order[:, None] == device_ids[None, :], device_ids[:, None], 0), axis=0
    )
    own_slot = jnp.sum(jnp.where(deal_order == own_index, device_ids, 0))
    first_clip = own_index * held
    own_blocks = lax.dynamic_slice(clip_blocks, (first_clip,), (held,))
    own_starts = lax.dynamic_slice(block_starts, (first_clip,), (held,))
    own_start = own_starts[0]
    turn = jnp.arange(capacity, dtype=jnp.int32)

    width = kernel.shape[1]
    lanes = -(-width // 128) * 128
    shards = gather(jnp.pad(kernel, ((0, 0), (0, lanes - width))), "slab", False, 0)
    rows_held = kernel.shape[0]
    own_rows = shards[:, :, :width].transpose(1, 0, 2).reshape(rows_held, out_channels, TAPS)
    taps = gather(own_rows.transpose(2, 0, 1), "clips", True, 1)
    taps = taps.reshape(TAPS, in_channels, out_channels)

    range_start = block_starts.reshape(clip_devs, held)[:, 0]
    range_end = block_ends.reshape(clip_devs, held)[:, held - 1]
    first_block = range_start + jnp.mod(own_slot - range_start, clip_devs)
    block_id = first_block[:, None] + turn[None, :] * clip_devs
    slot_of = jnp.where(block_id < range_end[:, None], block_id // clip_devs, -1).reshape(-1)
    slot_ids = jnp.arange(slot_count, dtype=jnp.int32)
    pieces = picked(slot_of[:, None] == slot_ids[None, :], cotangent)
    returned = lax.all_to_all(
        pieces.reshape((clip_devs, capacity) + pieces.shape[1:]),
        "clips",
        split_axis=0,
        concat_axis=0,
        tiled=True,
    )
    block_range = jnp.arange(BMAX, dtype=jnp.int32)[None, :]
    own_ids = own_starts[:, None] + block_range
    own_live = (block_range < own_blocks[:, None]).reshape(-1)
    source = jnp.sum(
        jnp.where(
            jnp.mod(own_ids, clip_devs).reshape(-1)[:, None] == device_ids[None, :],
            deal_order[None, :],
            0,
        ),
        axis=1,
    )
    came = source * capacity + (own_ids.reshape(-1) - own_start) // clip_devs
    came = jnp.where(own_live, came, -1)
    piece_ids = jnp.arange(clip_devs * capacity, dtype=jnp.int32)
    flat_rows = returned.reshape((clip_devs * capacity,) + returned.shape[2:])
    grad_act = picked(came[:, None] == piece_ids[None, :], flat_rows)
    cells = frames * row_count * columns
    grad_act = grad_act.reshape(held, cells, out_channels).astype(jnp.float32)

    rimmed = extended(video, "slab", 2)
    padded = jnp.pad(rimmed, ((0, 0), (2, 0), (0, 0), (1, 1), (0, 0)))
    side = nine(padded, columns, False)
    weights = taps.reshape(3, 9 * in_channels, out_channels)
    steps = [side[:, a : a + frames].reshape(held * cells, 9 * in_channels) for a in range(3)]
    conv = sum(
        jnp.dot(steps[a], weights[a], preferred_element_type=jnp.float32) for a in range(3)
    ).reshape(held, cells, out_channels)

    cell_frame = jnp.arange(cells, dtype=jnp.int32) // (row_count * columns)
    alive = (cell_frame[None, :] < (own_blocks * FB)[:, None])[:, :, None]
    channel = jnp.arange(out_channels, dtype=jnp.int32) // per_group
    same_group = (channel[:, None] == channel[None, :]).astype(jnp.float32)
    count = (own_blocks * (FB * row_count * slab_devs * columns * per_group)).astype(jnp.float32)
    count = count[:, None]
    live_conv = jnp.where(alive, conv, 0.0)
    rest = jnp.zeros((-(2 * held) % 8, out_channels), jnp.float32)

    def slab_sums(one, two, collective_id):
        packed = jnp.concatenate([one, two, rest], axis=0)
        (sums,) = reduce((packed,), (None,), "slab", collective_id)
        return sums

    def grouped(sums):
        return jnp.dot(sums, same_group, precision=highest)

    sums = grouped(slab_sums(jnp.sum(live_conv, 1), jnp.sum(live_conv * live_conv, 1), 2))
    mean = sums[:held] / count
    variance = sums[held : 2 * held] / count - mean * mean
    inv_std = lax.rsqrt(variance + 1e-05)
    normed = (conv - mean[:, None]) * inv_std[:, None]
    affine = normed * gain + bias
    sigmoid = jax.nn.sigmoid(affine)

    act = jax.nn.silu(affine).astype(jnp.bfloat16)
    act = act.reshape(held * BMAX, FB, row_count, columns, out_channels)
    own_end = own_starts[held - 1] + own_blocks[held - 1]
    first_block = own_start + jnp.mod(deal_slot - own_start, clip_devs)
    block_id = (first_block[:, None] + turn[None, :] * clip_devs).reshape(-1)
    wanted = (block_id[:, None] == own_ids.reshape(-1)[None, :]) & own_live[None, :]
    pieces = picked(wanted & (block_id < own_end)[:, None], act)
    received = lax.all_to_all(
        pieces.reshape((clip_devs, capacity) + pieces.shape[1:]),
        "clips",
        split_axis=0,
        concat_axis=0,
        tiled=True,
    )
    slot_blocks = slot_ids * clip_devs + own_slot
    slot_clip = jnp.sum((block_ends[None, :] <= slot_blocks[:, None]).astype(jnp.int32), axis=1)
    source = slot_clip // held
    source_start = jnp.sum(
        jnp.where(source[:, None] == device_ids[None, :], range_start[None, :], 0), axis=1
    )
    came = source * capacity + (slot_blocks - source_start) // clip_devs
    flat_rows = received.reshape((clip_devs * capacity,) + received.shape[2:])
    activations = picked(came[:, None] == piece_ids[None, :], flat_rows)

    grad_affine = grad_act * sigmoid * (1.0 + affine * (1.0 - sigmoid))
    sums = slab_sums(jnp.sum(grad_affine, 1), jnp.sum(grad_affine * normed, 1), 3)
    means = grouped(sums * gain)
    mean_grad = means[:held] / count
    mean_cross = means[held : 2 * held] / count
    grad_conv = inv_std[:, None] * (
        grad_affine * gain - mean_grad[:, None] - normed * mean_cross[:, None]
    )
    grad_conv = jnp.where(alive, grad_conv, 0.0).astype(jnp.bfloat16)
    bias_own = jnp.sum(sums[:held], axis=0, keepdims=True)
    gain_own = jnp.sum(sums[held : 2 * held], axis=0, keepdims=True)
    small = jnp.concatenate([bias_own, gain_own, jnp.zeros((6, out_channels), jnp.float32)], axis=0)

    grad_flat = grad_conv.reshape(held * cells, out_channels)
    terms = jnp.stack(
        [
            lax.dot_general(
                steps[a],
                grad_flat,
                (((0,), (0,)), ((), ())),
                preferred_element_type=jnp.float32,
            ).astype(jnp.bfloat16)
            for a in range(3)
        ]
    ).reshape(TAPS, clip_devs, rows_held, out_channels)
    rimmed_grad = extended(
        grad_conv.reshape(held, frames, row_count, columns, out_channels), "slab", 2
    )
    own_terms, small_sums = reduce((terms, small), (1, None), "clips", 4)
    own_terms = own_terms.transpose(1, 2, 0).reshape(rows_held, slab_devs, width)
    own_terms = jnp.pad(own_terms.transpose(1, 0, 2), ((0, 0), (0, 0), (0, lanes - width)))
    (kernel_grad,) = reduce((own_terms,), (0,), "slab", 5)

    grad_padded = jnp.pad(rimmed_grad, ((0, 0), (0, 2), (0, 0), (1, 1), (0, 0)))
    grad_side = nine(grad_padded, columns, True)
    turned = taps.reshape(3, 9, in_channels, out_channels).transpose(0, 1, 3, 2)
    turned = turned.reshape(3, 9 * out_channels, in_channels)
    video_grad = sum(
        jnp.dot(
            grad_side[:, 2 - a : 2 - a + frames].reshape(held * cells, 9 * out_channels),
            turned[a],
            preferred_element_type=jnp.float32,
        )
        for a in range(3)
    )
    video_grad = video_grad.reshape(video.shape).astype(jnp.bfloat16)
    return (activations, video_grad, kernel_grad[:, :width], small_sums[1], small_sums[0])


def solution(mesh):
    return jax.shard_map(
        body,
        mesh=mesh,
        in_specs=(
            P("clips", None, "slab", None, None),
            P(),
            P(),
            P("clips", "slab"),
            P(),
            P(),
            P("clips", None, "slab", None, None),
        ),
        out_specs=(
            P("clips", None, "slab", None, None),
            P("clips", None, "slab", None, None),
            P("clips", "slab"),
            P(),
            P(),
        ),
        check_vma=False,
    )
```

time: 645 us -> 229 us (0.36); the launches traced: 633 us -> 227 us
  blocking collectives: 232 us -> 0 us
  waiting for transfers between devices: 229 us -> 5.34 us
  Pallas kernels: 0 us -> 147 us
  matrix products: 52.1 us -> 6.02 us
  local copies, waits for them, and re-layouts: 66.3 us -> 20.4 us
  between operations: 15.4 us -> 2.7 us
  other arithmetic: 12.1 us -> 21.9 us
    psum x2 -> x0, blocking collectives: 205 us -> none  [the longest x1 104 us: body(): lax.psum((table_first, table_second), ('clips', 'slab'))]
    unnamed x5 -> x0, waiting for transfers between devices: 188 us -> none
    pallas_call x0 -> x6, Pallas kernels: none -> 147 us  [the longest x4 88.9 us: reduce(): pl.pallas_call(functools.partial(reduce_kernel, axis, n, parts), out_shap...]
    dot_general x89 -> x11, matrix products: 52.1 us -> 6.02 us  [the longest x2 1.73 us: grouped(): return jnp.dot(sums, same_group, precision=highest)]
    all_gather x1 -> x0, waiting for transfers between devices: 39.2 us -> none  [body(): full_kernel = lax.all_gather(full_kernel, 'clips', axis=0, tiled=True)]
    all_gather x1 -> x0, blocking collectives: 27.6 us -> none  [body(): full_kernel = lax.all_gather(kernel, 'slab', axis=1, tiled=True)]
    slice x35 -> x6, local copies, waits for them, and re-layouts: 27.4 us -> 5.59 us  [the longest x1 2.78 us: body(): weights[a]]
    all_to_all x1 -> x0, starting transfers between devices: 10.4 us -> none  [body(): lax.all_to_all(sent, 'clips', split_axis=0, concat_axis=0, tiled=True)]
  transfers between devices with their start and end apart: 9 -> 6, of which waited for: 5 -> 1; matrix products, arithmetic and copies ran while one was open for 9% -> 17% of each run, Pallas kernels for 0% -> 58%
where the time goes in v1:
time: 229 us; the launch traced here: 227 us
  Pallas kernels  147 us (64%)
  starting transfers between devices  24.3 us (11%)
  other arithmetic  21.9 us (10%)
  local copies, waits for them, and re-layouts  20.4 us (9%)
  matrix products  6.02 us (3%)
  waiting for transfers between devices  5.34 us (2%)
  between operations  2.7 us (1%)
    pallas_call x4, Pallas kernels, reduce(): pl.pallas_call(functools.partial(reduce_kernel, axis, n, parts), out_shap...  88.9 us
    pallas_call x2, Pallas kernels, gather(): pl.pallas_call(functools.partial(gather_kernel, axis, n, inner), out_shap...  57.9 us
    all_to_all x2, starting transfers between devices, body(): lax.all_to_all(pieces.reshape((clip_devs, capacity) + pieces.shape[1:]),...  13.5 us
    ppermute x2, starting transfers between devices, extended(): lax.ppermute(lax.slice_in_dim(array, length - 1, length, axis=dim), axis,...  8.22 us
    all_to_all x2, waiting for transfers between devices, body(): lax.all_to_all(pieces.reshape((clip_devs, capacity) + pieces.shape[1:]),...  5.33 us
    reduce_sum x4, other arithmetic, picked(): jnp.sum(jnp.where(mask, array[None], jnp.zeros((), array.dtype)), axis=1)  5.06 us
  transfers between devices with their start and end apart: 6, of which 1 were waited for; matrix products, arithmetic and copies ran while one was open for 17% of the time, Pallas kernels for 58%

profile of v1, /device:TPU:1, one launch (start us, length us, event | category | flops | bytes accessed | tf_op | source)
XLA Modules:
  0.0 227.4 jit_solution(17962108282918466052)
XLA Ops:
  0.6 5.0 %collective-permute-start = (bf16[2,6,1,16,256]{4,3,2,1,0:T(8,128)(2,1)}, bf16[2,6,1,16,256]{4,3,2,1,0:T(8,128)(2,1)}, u32[]{:S(2)}, u32[]{:S(2)}) collective-permute-start(bf16[2,6,1,16,256]{4,3,2,1,0:T(8,128)(2,1)} %param.7), channel_id=1, source_target_pairs={{0,1},{1,2},{2,3},{3,4},{4,5},{5,6},{6,7},{7,8},{8,9},{9,10},{10,1... | collective-permute-start | bytes 294920 | tf_op jit(solution)/shard_map/ppermute | solution.py:21
  5.6 1.3 collective-permute-start.1
  8.8 1.3 fusion.65
  10.1 1.3 fusion.59
  11.4 1.8 select_reduce_fusion.2
  13.2 8.1 %all-to-all-start.1 = ((bf16[32,1,2,1,16,128]{5,4,2,3,1,0:T(8,128)(2,1)}), bf16[32,1,2,1,16,128]{5,4,2,3,1,0:T(8,128)(2,1)}, u32[]{:S(2)}, u32[]{:S(2)}) async-start(bf16[32,1,2,1,16,128]{5,4,2,3,1,0:T(8,128)(2,1)} %bitcast.29), calls=%async_computation.1 | async-start | bytes 524288 | tf_op jit(solution)/shard_map/all_to_all | solution.py:205
  23.5 1.3 select_reduce_fusion.5
  24.8 1.2 multiply_add_fusion.2
  26.0 1.3 pad.17.x_ref
  27.3 21.5 %shard_map.110 = bf16[16,8,256]{2,1,0:T(8,128)(2,1)} custom-call(bf16[8,256]{1,0:T(8,128)(2,1)} %pad.17.x_ref), custom_call_target="tpu_custom_call" | custom-call | tf_op jit(solution)/shard_map/pallas_call | solution.py:76
  50.6 36.4 %shard_map.111 = bf16[27,32,8,128]{3,2,1,0:T(8,128)(2,1)} custom-call(bf16[27,8,128]{2,1,0:T(8,128)(2,1)} %bitcast.222), custom_call_target="tpu_custom_call" | custom-call | tf_op jit(solution)/shard_map/pallas_call | solution.py:76
  87.0 2.8 %fusion.73 = (bf16[9,32,8,128]{3,2,1,0:T(8,128)(2,1)}, bf16[9,32,8,128]{3,2,1,0:T(8,128)(2,1)}, bf16[9,32,8,128]{3,2,1,0:T(8,128)(2,1)}) fusion(bf16[27,32,8,128]{3,2,1,0:T(8,128)(2,1)} %shard_map.111), kind=kLoop, calls=%fused_computation.199 | loop fusion | bytes 3538944 | tf_op jit(solution)/shard_map/slice | solution.py:237
  94.2 0.9 copy.84
  95.2 1.3 fusion.72
  99.8 1.2 fusion.11
  105.0 14.7 %shard_map.112 = f32[8,128]{1,0:T(8,128)} custom-call(f32[8,128]{1,0:T(8,128)} %maximum_maximum_fusion.refs_0_), custom_call_target="tpu_custom_call" | custom-call | tf_op jit(solution)/shard_map/pallas_call | solution.py:143
  119.7 0.9 fusion.40
  120.7 1.3 select_reduce_fusion
  122.9 14.4 %shard_map.113 = f32[8,128]{1,0:T(8,128)} custom-call(f32[8,128]{1,0:T(8,128)} %maximum_maximum_fusion.1.refs_0_), custom_call_target="tpu_custom_call" | custom-call | tf_op jit(solution)/shard_map/pallas_call | solution.py:143
  138.1 0.9 fusion.38
  140.9 3.2 %collective-permute-start.2 = (bf16[2,6,1,16,128]{4,3,1,0,2:T(8,128)(2,1)S(1)}, bf16[2,6,1,16,128]{4,3,1,0,2:T(8,128)(2,1)S(1)}, u32[]{:S(2)}, u32[]{:S(2)}) collective-permute-start(bf16[2,6,1,16,128]{4,3,1,0,2:T(8,128)(2,1)S(1)} %select_convert_fusion), channel_id=1, source_target_pairs={{0,1},{1,2},{2,3},{3,4},{4,5},{5,6},{6,7},{7,8},{8,9},{9,10},{10,1... | collective-permute-start | bytes 147464 | tf_op jit(solution)/shard_map/ppermute | solution.py:21
  144.1 1.3 collective-permute-start.3
  146.1 1.4 pad_maximum_fusion
  147.5 38.2 %shard_map.114 = (f32[27,8,128]{2,1,0:T(8,128)}, f32[8,128]{1,0:T(8,128)}) custom-call(bf16[27,32,8,128]{3,2,1,0:T(8,128)(2,1)} %bitcast.205, f32[8,128]{1,0:T(8,128)} %maximum_maximum_fusion.2.refs_1_), custom_call_target="tpu_custom_call" | custom-call | tf_op jit(solution)/shard_map/pallas_call | solution.py:143
  185.7 1.3 slice_bitcast_fusion.19
  186.9 1.1 select_reduce_fusion.1
  188.1 1.1 copy.85
  190.1 21.5 %shard_map.115 = f32[8,256]{1,0:T(8,128)} custom-call(f32[16,8,256]{2,1,0:T(8,128)} %pad.19.refs_0_), custom_call_target="tpu_custom_call" | custom-call | tf_op jit(solution)/shard_map/pallas_call | solution.py:143
  211.7 5.4 %all-to-all-start = ((bf16[32,1,2,1,16,128]{5,4,2,3,1,0:T(8,128)(2,1)}), bf16[32,1,2,1,16,128]{5,4,2,3,1,0:T(8,128)(2,1)S(1)}, u32[]{:S(2)}, u32[]{:S(2)}) async-start(bf16[32,1,2,1,16,128]{5,4,2,3,1,0:T(8,128)(2,1)} %bitcast.23), calls=%async_computation | async-start | bytes 524288 | tf_op jit(solution)/shard_map/all_to_all | solution.py:272
  217.7 0.9 copy-done.4
  219.7 0.9 fusion.8
  220.7 5.3 %all-to-all-done = bf16[32,1,2,1,16,128]{5,4,2,3,1,0:T(8,128)(2,1)S(1)} async-done(((bf16[32,1,2,1,16,128]{5,4,2,3,1,0:T(8,128)(2,1)}), bf16[32,1,2,1,16,128]{5,4,2,3,1,0:T(8,128)(2,1)S(1)}, u32[]{:S(2)}, u32[]{:S(2)}) %all-to-all-start) | async-done | bytes 262176 | tf_op jit(solution)/shard_map/all_to_all | solution.py:272
  (154 shorter events, 24.4 us)
Async XLA Ops:
  0.6 99.1 %collective-permute-start = (bf16[2,6,1,16,256]{4,3,2,1,0:T(8,128)(2,1)}, bf16[2,6,1,16,256]{4,3,2,1,0:T(8,128)(2,1)}, u32[]{:S(2)}, u32[]{:S(2)}) collective-permute-start(bf16[2,6,1,16,256]{4,3,2,1,0:T(8,128)(2,1)} %param.7), channel_id=1, source_target_pairs={{0,1},{1,2},{2,3},{3,4},{4,5},{5,6},{6,7},{7,8},{8,9},{9,10},{10,1... | collective-permute-start | bytes 294920 | tf_op jit(solution)/shard_map/ppermute | solution.py:21
  5.6 94.1 %collective-permute-start.1 = (bf16[2,6,1,16,256]{4,3,2,1,0:T(8,128)(2,1)}, bf16[2,6,1,16,256]{4,3,2,1,0:T(8,128)(2,1)}, u32[]{:S(2)}, u32[]{:S(2)}) collective-permute-start(bf16[2,6,1,16,256]{4,3,2,1,0:T(8,128)(2,1)} %param.7), channel_id=1, source_target_pairs={{1,0},{2,1},{3,2},{4,3},{5,4},{6,5},{7,6},{8,7},{9,8},{10,9},{11,1... | collective-permute-start | bytes 294920 | tf_op jit(solution)/shard_map/ppermute | solution.py:22
  7.9 19.4 %copy-start.12 = (s32[64]{0:T(128)}, s32[64]{0:T(128)S(1)}, u32[]{:S(2)}) copy-start(s32[64]{0:T(128)S(1)} %reduce.14) | copy-start | bytes 772
  13.2 107.5 %all-to-all-start.1 = ((bf16[32,1,2,1,16,128]{5,4,2,3,1,0:T(8,128)(2,1)}), bf16[32,1,2,1,16,128]{5,4,2,3,1,0:T(8,128)(2,1)}, u32[]{:S(2)}, u32[]{:S(2)}) async-start(bf16[32,1,2,1,16,128]{5,4,2,3,1,0:T(8,128)(2,1)} %bitcast.29), calls=%async_computation.1 | async-start | bytes 524288 | tf_op jit(solution)/shard_map/all_to_all | solution.py:205
  87.0 3.5 %copy-start.24 = (s32[32]{0:T(128)S(1)}, s32[32]{0:T(128)}, u32[]{:S(2)}) copy-start(s32[32]{0:T(128)} %param.9) | copy-start | bytes 388
  87.0 7.2 %copy-start = (bf16[27,32,8,128]{3,2,1,0:T(8,128)(2,1)S(1)}, bf16[27,32,8,128]{3,2,1,0:T(8,128)(2,1)}, u32[]{:S(2)}) copy-start(bf16[27,32,8,128]{3,2,1,0:T(8,128)(2,1)} %shard_map.111) | copy-start | bytes 5308420
  90.5 3.0 %copy-start.14 = (s32[6]{0:T(128)}, s32[6]{0:T(128)S(1)}, u32[]{:S(2)}) copy-start(s32[6]{0:T(128)S(1)} %add.274) | copy-start | bytes 76
  90.8 3.4 %copy-start.16 = (pred[6]{0:T(512)(128)(4,1)}, pred[6]{0:T(512)(128)(4,1)S(1)}, u32[]{:S(2)}) copy-start(pred[6]{0:T(512)(128)(4,1)S(1)} %lt.93) | copy-start | bytes 22
  95.1 2.6 %copy-start.22 = (s32[32]{0:T(128)S(1)}, s32[32]{0:T(128)}, u32[]{:S(2)}) copy-start(s32[32]{0:T(128)} %select_reduce_fusion.5) | copy-start | bytes 388
  95.1 3.3 %copy-start.15 = (s32[6]{0:T(128)S(1)}, s32[6]{0:T(128)}, u32[]{:S(2)}) copy-start(s32[6]{0:T(128)} %copy-done.14) | copy-start | bytes 76
  95.1 3.3 %copy-start.17 = (pred[6]{0:T(512)(128)(4,1)S(1)}, pred[6]{0:T(512)(128)(4,1)}, u32[]{:S(2)}) copy-start(pred[6]{0:T(512)(128)(4,1)} %copy-done.16) | copy-start | bytes 22
  95.1 3.5 %copy-start.13 = (s32[64]{0:T(128)S(1)}, s32[64]{0:T(128)}, u32[]{:S(2)}) copy-start(s32[64]{0:T(128)} %copy-done.12) | copy-start | bytes 772
  95.2 3.5 %copy-start.25 = (s32[4]{0:T(128)S(1)}, s32[4]{0:T(128)}, u32[]{:S(2)}) copy-start(s32[4]{0:T(128)} %multiply_add_fusion.2) | copy-start | bytes 52
  95.2 3.6 %copy-start.20 = (s32[32]{0:T(128)S(1)}, s32[32]{0:T(128)}, u32[]{:S(2)}) copy-start(s32[32]{0:T(128)} %get-tuple-element.39) | copy-start | bytes 388
  95.2 4.6 %copy-start.11 = (s32[192]{0:T(256)S(1)}, s32[192]{0:T(256)}, u32[]{:S(2)}) copy-start(s32[192]{0:T(256)} %lt.106) | copy-start | bytes 2308
  95.2 4.6 %copy-start.7 = (bf16[2,6,1,16,256]{4,3,2,1,0:T(8,128)(2,1)S(1)}, bf16[2,6,1,16,256]{4,3,2,1,0:T(8,128)(2,1)}, u32[]{:S(2)}) copy-start(bf16[2,6,1,16,256]{4,3,2,1,0:T(8,128)(2,1)} %param.7) | copy-start | bytes 294916
  101.3 1.1 copy-start.3
  101.5 1.2 copy-start.2
  102.8 1.1 copy-start.1
  103.2 1.0 copy-start.21
  103.2 1.2 copy-start.18
  103.2 17.5 %copy-start.19 = (pred[6,32]{1,0:T(8,128)(4,1)S(1)}, pred[6,32]{1,0:T(8,128)(4,1)}, u32[]{:S(2)}) copy-start(pred[6,32]{1,0:T(8,128)(4,1)} %iota_compare_fusion.8) | copy-start | bytes 580
  103.2 18.8 %copy-start.9 = (f32[128]{0:T(128)S(1)}, f32[128]{0:T(128)}, u32[]{:S(2)}) copy-start(f32[128]{0:T(128)} %param.12) | copy-start | bytes 1540
  103.2 18.8 %copy-start.10 = (f32[128]{0:T(128)S(1)}, f32[128]{0:T(128)}, u32[]{:S(2)}) copy-start(f32[128]{0:T(128)} %param.11) | copy-start | bytes 1540
  140.2 5.2 %copy-start.23 = (f32[8]{0:T(128)S(1)}, f32[8]{0:T(128)}, u32[]{:S(2)}) copy-start(f32[8]{0:T(128)} %pad.22.clone) | copy-start | bytes 100
  140.9 76.3 %collective-permute-start.2 = (bf16[2,6,1,16,128]{4,3,1,0,2:T(8,128)(2,1)S(1)}, bf16[2,6,1,16,128]{4,3,1,0,2:T(8,128)(2,1)S(1)}, u32[]{:S(2)}, u32[]{:S(2)}) collective-permute-start(bf16[2,6,1,16,128]{4,3,1,0,2:T(8,128)(2,1)S(1)} %select_convert_fusion), channel_id=1, source_target_pairs={{0,1},{1,2},{2,3},{3,4},{4,5},{5,6},{6,7},{7,8},{8,9},{9,10},{10,1... | collective-permute-start | bytes 147464 | tf_op jit(solution)/shard_map/ppermute | solution.py:21
  144.1 73.0 %collective-permute-start.3 = (bf16[2,6,1,16,128]{4,3,1,0,2:T(8,128)(2,1)S(1)}, bf16[2,6,1,16,128]{4,3,1,0,2:T(8,128)(2,1)S(1)}, u32[]{:S(2)}, u32[]{:S(2)}) collective-permute-start(bf16[2,6,1,16,128]{4,3,1,0,2:T(8,128)(2,1)S(1)} %select_convert_fusion), channel_id=1, source_target_pairs={{1,0},{2,1},{3,2},{4,3},{5,4},{6,5},{7,6},{8,7},{9,8},{10,9},{11,1... | collective-permute-start | bytes 147464 | tf_op jit(solution)/shard_map/ppermute | solution.py:22
  211.7 14.3 %all-to-all-start = ((bf16[32,1,2,1,16,128]{5,4,2,3,1,0:T(8,128)(2,1)}), bf16[32,1,2,1,16,128]{5,4,2,3,1,0:T(8,128)(2,1)S(1)}, u32[]{:S(2)}, u32[]{:S(2)}) async-start(bf16[32,1,2,1,16,128]{5,4,2,3,1,0:T(8,128)(2,1)} %bitcast.23), calls=%async_computation | async-start | bytes 524288 | tf_op jit(solution)/shard_map/all_to_all | solution.py:272
  217.6 1.1 copy-start.4
  217.7 1.3 copy-start.6
  218.6 1.1 copy-start.5
  218.9 7.9 %copy-start.8 = (f32[8,256]{1,0:T(8,128)S(1)}, f32[8,256]{1,0:T(8,128)}, u32[]{:S(2)}) copy-start(f32[8,256]{1,0:T(8,128)} %shard_map.115) | copy-start | bytes 24580

commit v2 on v1

--- a/solution.py
+++ b/solution.py
@@ -152,6 +152,245 @@
     )(*xs)
 
 
+def loop(low, high, step):
+    def once(k, carry):
+        step(k)
+        return carry
+
+    lax.fori_loop(low, high, once, 0)
+
+
+def weights_kernel(n, x_ref, y_ref, out_ref, land_ref, sems, y_sems, own):
+    me = lax.axis_index("clips")
+    greet("clips", n, me)
+    chips = n // 2
+    partner = me + 1 - 2 * lax.rem(me, 2)
+
+    def direct(j):
+        peer = lax.rem(me + 2 * j, n)
+        return remote("clips", peer, x_ref, out_ref.at[:, me], sems.at[0], sems.at[1], j)
+
+    def passed(j):
+        place = out_ref.at[:, lax.rem(me + n - 2 * j, n)]
+        return remote("clips", partner, place, place, sems.at[2], sems.at[3], j)
+
+    def first():
+        return remote("clips", partner, x_ref, out_ref.at[:, me], sems.at[2], sems.at[3], 0)
+
+    def other(k):
+        peer = lax.rem(me + k, n)
+        return remote(
+            "clips", peer, y_ref.at[peer], land_ref.at[me], y_sems.at[0], y_sems.at[1], k
+        )
+
+    loop(1, chips, lambda j: direct(j).start())
+    first().start()
+    loop(1, n, lambda k: other(k).start())
+    for source, target in ((x_ref, out_ref.at[:, me]), (y_ref.at[me], land_ref.at[me])):
+        local = pltpu.make_async_copy(source, target, own)
+        local.start()
+        local.wait()
+
+    def relay(j):
+        direct(j).wait_recv()
+        passed(j).start()
+
+    loop(1, chips, relay)
+    loop(1, chips, lambda j: direct(j).wait_send())
+    first().wait()
+    loop(1, chips, lambda j: passed(j).wait())
+    loop(1, n, lambda k: other(k).wait())
+
+
+def weights_gather(x, y, collective_id):
+    n = lax.axis_size("clips")
+    vmem = pl.BlockSpec(memory_space=pltpu.VMEM)
+    return pl.pallas_call(
+        functools.partial(weights_kernel, n),
+        out_shape=[
+            jax.ShapeDtypeStruct((x.shape[0], n) + x.shape[1:], x.dtype),
+            jax.ShapeDtypeStruct(y.shape, y.dtype),
+        ],
+        in_specs=[vmem] * 2,
+        out_specs=[vmem] * 2,
+        scratch_shapes=[
+            pltpu.SemaphoreType.DMA((4, n // 2)),
+            pltpu.SemaphoreType.DMA((2, n)),
+            pltpu.SemaphoreType.DMA,
+        ],
+        compiler_params=pltpu.CompilerParams(collective_id=collective_id, has_side_effects=True),
+    )(x, y)
+
+
+def terms_kernel(
+    n, x_ref, s_ref, y_ref, out_ref, sum_ref, land_ref, half, mixed, held, shelf, sems, o_sems, own
+):
+    me = lax.axis_index("clips")
+    greet("clips", n, me)
+    chips = n // 2
+    core, chip = lax.rem(me, 2), me // 2
+    partner = me + 1 - 2 * core
+
+    def near(j):
+        c = lax.rem(chip + j, chips)
+        return remote(
+            "clips", partner, x_ref.at[:, c, 1 - core], half.at[c], sems.at[0], sems.at[1], j
+        )
+
+    def far(j):
+        c = lax.rem(chip + j, chips)
+        return remote(
+            "clips", 2 * c + core, mixed.at[c], held.at[chip], sems.at[2], sems.at[3], j
+        )
+
+    def summed(k):
+        peer = lax.rem(me + k, n)
+        return remote("clips", peer, s_ref, shelf.at[me], o_sems.at[0], o_sems.at[1], k)
+
+    def other(k):
+        peer = lax.rem(me + k, n)
+        return remote(
+            "clips", peer, y_ref.at[peer], land_ref.at[me], o_sems.at[2], o_sems.at[3], k
+        )
+
+    loop(0, chips, lambda j: near(j).start())
+
+    def mix(j):
+        c = lax.rem(chip + j, chips)
+        near(j).wait_recv()
+        both = x_ref[:, c, core].astype(jnp.float32) + half[c].astype(jnp.float32)
+        mixed[c] = both.astype(jnp.bfloat16)
+        far(j).start()
+
+    loop(1, chips, mix)
+    loop(1, n, lambda k: summed(k).start())
+    loop(1, n, lambda k: other(k).start())
+    for source, target in ((s_ref, shelf.at[me]), (y_ref.at[me], land_ref.at[me])):
+        local = pltpu.make_async_copy(source, target, own)
+        local.start()
+        local.wait()
+    near(0).wait_recv()
+    out_ref[...] = x_ref[:, chip, core].astype(jnp.float32) + half[chip].astype(jnp.float32)
+
+    def add(j):
+        far(j).wait_recv()
+        out_ref[...] += held[lax.rem(chip + chips - j, chips)].astype(jnp.float32)
+
+    loop(1, chips, add)
+    loop(0, chips, lambda j: near(j).wait_send())
+    loop(1, chips, lambda j: far(j).wait_send())
+    loop(1, n, lambda k: summed(k).wait())
+    loop(1, n, lambda k: other(k).wait())
+    sum_ref[...] = jnp.zeros(sum_ref.shape, jnp.float32)
+
+    def total(k):
+        sum_ref[...] += shelf[k]
+
+    loop(0, n, total)
+
+
+def terms_reduce(x, s, y, collective_id):
+    n = lax.axis_size("clips")
+    vmem = pl.BlockSpec(memory_space=pltpu.VMEM)
+    shape = (x.shape[0],) + x.shape[3:]
+    return pl.pallas_call(
+        functools.partial(terms_kernel, n),
+        out_shape=[
+            jax.ShapeDtypeStruct(shape, jnp.float32),
+            jax.ShapeDtypeStruct(s.shape, s.dtype),
+            jax.ShapeDtypeStruct(y.shape, y.dtype),
+        ],
+        in_specs=[vmem] * 3,
+        out_specs=[vmem] * 3,
+        scratch_shapes=[pltpu.VMEM((n // 2,) + shape, x.dtype)] * 3
+        + [
+            pltpu.VMEM((n,) + s.shape, s.dtype),
+            pltpu.SemaphoreType.DMA((4, n // 2)),
+            pltpu.SemaphoreType.DMA((4, n)),
+            pltpu.SemaphoreType.DMA,
+        ],
+        compiler_params=pltpu.CompilerParams(collective_id=collective_id, has_side_effects=True),
+    )(x, s, y)
+
+
+def norm_kernel(
+    n, clips, conv_ref, grad_ref, alive_ref, count_ref, gain_ref, bias_ref, group_ref,
+    act_ref, out_ref, sum_ref, one, two, shelf_one, shelf_two, sems, own,
+):
+    me = lax.axis_index("slab")
+    greet("slab", n, me)
+
+    def total(rows, packed, shelf, base):
+        packed[...] = jnp.concatenate(rows, axis=0)
+
+        def copy(k):
+            peer = lax.rem(me + k, n)
+            return remote("slab", peer, packed, shelf.at[me], sems.at[base], sems.at[base + 1], k)
+
+        loop(1, n, lambda k: copy(k).start())
+        local = pltpu.make_async_copy(packed, shelf.at[me], own)
+        local.start()
+        local.wait()
+        loop(1, n, lambda k: copy(k).wait())
+        return jnp.sum(shelf[...], axis=0)
+
+    def grouped(sums):
+        return jnp.dot(
+            sums,
+            group_ref[...],
+            precision=lax.Precision.HIGHEST,
+            preferred_element_type=jnp.float32,
+        ) / count_ref[...]
+
+    def rows_of(parts):
+        rows = [jnp.sum(part, axis=0, keepdims=True) for part in parts]
+        return rows + [jnp.zeros((-len(parts) % 8, gain_ref.shape[1]), jnp.float32)]
+
+    gain, bias = gain_ref[...], bias_ref[...]
+    convs = [conv_ref[c] for c in range(clips)]
+    lives = [conv_ref[c] * alive_ref[c] for c in range(clips)]
+    means = grouped(total(rows_of(lives + [x * x for x in lives]), one, shelf_one, 0))
+    normed, grads, inverse = [], [], []
+    for c in range(clips):
+        mean = means[c : c + 1]
+        inv_std = lax.rsqrt(means[clips + c : clips + c + 1] - mean * mean + 1e-05)
+        inverse.append(inv_std)
+        normed.append((convs[c] - mean) * inv_std)
+        affine = normed[c] * gain + bias
+        sigmoid = jax.nn.sigmoid(affine)
+        act_ref[c] = (affine * sigmoid).astype(act_ref.dtype)
+        grads.append(grad_ref[c] * sigmoid * (1.0 + affine * (1.0 - sigmoid)))
+    sums = total(
+        rows_of(grads + [g * x for g, x in zip(grads, normed)]), two, shelf_two, 2
+    )
+    sum_ref[...] = sums
+    means = grouped(sums * gain)
+    for c in range(clips):
+        mean, cross = means[c : c + 1], means[clips + c : clips + c + 1]
+        grad = inverse[c] * (grads[c] * gain - mean - normed[c] * cross)
+        out_ref[c] = (grad * alive_ref[c]).astype(out_ref.dtype)
+
+
+def normalized(conv, grad, alive, count, gain, bias, group, collective_id):
+    n = lax.axis_size("slab")
+    vmem = pl.BlockSpec(memory_space=pltpu.VMEM)
+    rows = count.shape
+    return pl.pallas_call(
+        functools.partial(norm_kernel, n, conv.shape[0]),
+        out_shape=[
+            jax.ShapeDtypeStruct(conv.shape, jnp.bfloat16),
+            jax.ShapeDtypeStruct(conv.shape, jnp.bfloat16),
+            jax.ShapeDtypeStruct(rows, jnp.float32),
+        ],
+        in_specs=[vmem] * 7,
+        out_specs=[vmem] * 3,
+        scratch_shapes=[pltpu.VMEM(rows, jnp.float32)] * 2
+        + [pltpu.VMEM((n,) + rows, jnp.float32)] * 2
+        + [pltpu.SemaphoreType.DMA((4, n)), pltpu.SemaphoreType.DMA],
+        compiler_params=pltpu.CompilerParams(collective_id=collective_id, has_side_effects=True),
+    )(conv, grad, alive, count, gain, bias, group)
+
+
 def picked(mask, array):
     mask = mask.reshape(mask.shape + (1,) * (array.ndim - 1))
     return jnp.sum(jnp.where(mask, array[None], jnp.zeros((), array.dtype)), axis=1)
@@ -173,7 +412,6 @@
     out_channels = gain.shape[0]
     per_group = out_channels // GROUPS
     capacity = -(-(held * BMAX) // clip_devs)
-    highest = lax.Precision.HIGHEST
     block_ends = jnp.cumsum(clip_blocks)
     block_starts = block_ends - clip_blocks
     device_ids = jnp.arange(clip_devs, dtype=jnp.int32)
@@ -192,8 +430,6 @@
     shards = gather(jnp.pad(kernel, ((0, 0), (0, lanes - width))), "slab", False, 0)
     rows_held = kernel.shape[0]
     own_rows = shards[:, :, :width].transpose(1, 0, 2).reshape(rows_held, out_channels, TAPS)
-    taps = gather(own_rows.transpose(2, 0, 1), "clips", True, 1)
-    taps = taps.reshape(TAPS, in_channels, out_channels)
 
     range_start = block_starts.reshape(clip_devs, held)[:, 0]
     range_end = block_ends.reshape(clip_devs, held)[:, held - 1]
@@ -202,13 +438,10 @@
     slot_of = jnp.where(block_id < range_end[:, None], block_id // clip_devs, -1).reshape(-1)
     slot_ids = jnp.arange(slot_count, dtype=jnp.int32)
     pieces = picked(slot_of[:, None] == slot_ids[None, :], cotangent)
-    returned = lax.all_to_all(
-        pieces.reshape((clip_devs, capacity) + pieces.shape[1:]),
-        "clips",
-        split_axis=0,
-        concat_axis=0,
-        tiled=True,
-    )
+    block_cells = FB * row_count * columns
+    pieces = pieces.reshape(clip_devs, capacity * block_cells, out_channels)
+    taps, returned = weights_gather(own_rows.transpose(2, 0, 1), pieces, 1)
+    taps = taps.reshape(TAPS, in_channels, out_channels)
     block_range = jnp.arange(BMAX, dtype=jnp.int32)[None, :]
     own_ids = own_starts[:, None] + block_range
     own_live = (block_range < own_blocks[:, None]).reshape(-1)
@@ -223,7 +456,7 @@
     came = source * capacity + (own_ids.reshape(-1) - own_start) // clip_devs
     came = jnp.where(own_live, came, -1)
     piece_ids = jnp.arange(clip_devs * capacity, dtype=jnp.int32)
-    flat_rows = returned.reshape((clip_devs * capacity,) + returned.shape[2:])
+    flat_rows = returned.reshape(clip_devs * capacity, block_cells, out_channels)
     grad_act = picked(came[:, None] == piece_ids[None, :], flat_rows)
     cells = frames * row_count * columns
     grad_act = grad_act.reshape(held, cells, out_channels).astype(jnp.float32)
@@ -242,40 +475,29 @@
     channel = jnp.arange(out_channels, dtype=jnp.int32) // per_group
     same_group = (channel[:, None] == channel[None, :]).astype(jnp.float32)
     count = (own_blocks * (FB * row_count * slab_devs * columns * per_group)).astype(jnp.float32)
-    count = count[:, None]
-    live_conv = jnp.where(alive, conv, 0.0)
-    rest = jnp.zeros((-(2 * held) % 8, out_channels), jnp.float32)
-
-    def slab_sums(one, two, collective_id):
-        packed = jnp.concatenate([one, two, rest], axis=0)
-        (sums,) = reduce((packed,), (None,), "slab", collective_id)
-        return sums
-
-    def grouped(sums):
-        return jnp.dot(sums, same_group, precision=highest)
-
-    sums = grouped(slab_sums(jnp.sum(live_conv, 1), jnp.sum(live_conv * live_conv, 1), 2))
-    mean = sums[:held] / count
-    variance = sums[held : 2 * held] / count - mean * mean
-    inv_std = lax.rsqrt(variance + 1e-05)
-    normed = (conv - mean[:, None]) * inv_std[:, None]
-    affine = normed * gain + bias
-    sigmoid = jax.nn.sigmoid(affine)
-
-    act = jax.nn.silu(affine).astype(jnp.bfloat16)
-    act = act.reshape(held * BMAX, FB, row_count, columns, out_channels)
+    padding = jnp.ones((-(2 * held) % 8,), jnp.float32)
+    count = jnp.broadcast_to(
+        jnp.concatenate([count, count, padding])[:, None], (2 * held + padding.size, out_channels)
+    )
+    shape = (held, cells, out_channels)
+    act, grad_conv, sums = normalized(
+        conv,
+        grad_act,
+        jnp.broadcast_to(alive.astype(jnp.float32), shape),
+        count,
+        gain[None],
+        bias[None],
+        same_group,
+        2,
+    )
+
+    act = act.reshape(held * BMAX, block_cells, out_channels)
     own_end = own_starts[held - 1] + own_blocks[held - 1]
     first_block = own_start + jnp.mod(deal_slot - own_start, clip_devs)
     block_id = (first_block[:, None] + turn[None, :] * clip_devs).reshape(-1)
     wanted = (block_id[:, None] == own_ids.reshape(-1)[None, :]) & own_live[None, :]
     pieces = picked(wanted & (block_id < own_end)[:, None], act)
-    received = lax.all_to_all(
-        pieces.reshape((clip_devs, capacity) + pieces.shape[1:]),
-        "clips",
-        split_axis=0,
-        concat_axis=0,
-        tiled=True,
-    )
+    act_pieces = pieces.reshape(clip_devs, capacity * block_cells, out_channels)
     slot_blocks = slot_ids * clip_devs + own_slot
     slot_clip = jnp.sum((block_ends[None, :] <= slot_blocks[:, None]).astype(jnp.int32), axis=1)
     source = slot_clip // held
@@ -283,18 +505,6 @@
         jnp.where(source[:, None] == device_ids[None, :], range_start[None, :], 0), axis=1
     )
     came = source * capacity + (slot_blocks - source_start) // clip_devs
-    flat_rows = received.reshape((clip_devs * capacity,) + received.shape[2:])
-    activations = picked(came[:, None] == piece_ids[None, :], flat_rows)
-
-    grad_affine = grad_act * sigmoid * (1.0 + affine * (1.0 - sigmoid))
-    sums = slab_sums(jnp.sum(grad_affine, 1), jnp.sum(grad_affine * normed, 1), 3)
-    means = grouped(sums * gain)
-    mean_grad = means[:held] / count
-    mean_cross = means[held : 2 * held] / count
-    grad_conv = inv_std[:, None] * (
-        grad_affine * gain - mean_grad[:, None] - normed * mean_cross[:, None]
-    )
-    grad_conv = jnp.where(alive, grad_conv, 0.0).astype(jnp.bfloat16)
     bias_own = jnp.sum(sums[:held], axis=0, keepdims=True)
     gain_own = jnp.sum(sums[held : 2 * held], axis=0, keepdims=True)
     small = jnp.concatenate([bias_own, gain_own, jnp.zeros((6, out_channels), jnp.float32)], axis=0)
@@ -310,11 +520,14 @@
             ).astype(jnp.bfloat16)
             for a in range(3)
         ]
-    ).reshape(TAPS, clip_devs, rows_held, out_channels)
+    ).reshape(TAPS, clip_devs // 2, 2, rows_held, out_channels)
     rimmed_grad = extended(
         grad_conv.reshape(held, frames, row_count, columns, out_channels), "slab", 2
     )
-    own_terms, small_sums = reduce((terms, small), (1, None), "clips", 4)
+    own_terms, small_sums, received = terms_reduce(terms, small, act_pieces, 4)
+    flat_rows = received.reshape(clip_devs * capacity, block_cells, out_channels)
+    activations = picked(came[:, None] == piece_ids[None, :], flat_rows)
+    activations = activations.reshape(cotangent.shape)
     own_terms = own_terms.transpose(1, 2, 0).reshape(rows_held, slab_devs, width)
     own_terms = jnp.pad(own_terms.transpose(1, 0, 2), ((0, 0), (0, 0), (0, lanes - width)))
     (kernel_grad,) = reduce((own_terms,), (0,), "slab", 5)

time: 229 us -> 181 us (0.79)
  Pallas kernels: 147 us -> 122 us
  starting transfers between devices: 24.3 us -> 12.2 us
  waiting for transfers between devices: 5.34 us -> 0.01 us
  other arithmetic: 21.9 us -> 17.8 us
    pallas_call x0 -> x3, Pallas kernels: none -> 83.3 us  [the longest x1 30 us: terms_reduce(): pl.pallas_call(functools.partial(terms_kernel, n), out_shape=[jax.ShapeDt...]
    pallas_call x4 -> x1, Pallas kernels: 88.9 us -> 17.8 us  [reduce(): pl.pallas_call(functools.partial(reduce_kernel, axis, n, parts), out_shap...]
    pallas_call x2 -> x1, Pallas kernels: 57.9 us -> 20.5 us  [gather(): pl.pallas_call(functools.partial(gather_kernel, axis, n, inner), out_shap...]
    all_to_all x2 -> x0, starting transfers between devices: 13.5 us -> none  [body(): lax.all_to_all(pieces.reshape((clip_devs, capacity) + pieces.shape[1:]),...]
    all_to_all x2 -> x0, waiting for transfers between devices: 5.33 us -> none  [body(): lax.all_to_all(pieces.reshape((clip_devs, capacity) + pieces.shape[1:]),...]
  transfers between devices with their start and end apart: 6 -> 4, of which waited for: 1 -> 0; matrix products, arithmetic and copies ran while one was open for 17% -> 17% of each run, Pallas kernels for 58% -> 53%
where the time goes in v2:
time: 181 us; the launch traced here: 180 us
  Pallas kernels  122 us (67%)
  local copies, waits for them, and re-layouts  19.8 us (11%)
  other arithmetic  17.8 us (10%)
  starting transfers between devices  12.2 us (7%)
  matrix products  5.79 us (3%)
  between operations  2.5 us (1%)
    pallas_call x1, Pallas kernels, terms_reduce(): pl.pallas_call(functools.partial(terms_kernel, n), out_shape=[jax.ShapeDt...  30 us
    pallas_call x1, Pallas kernels, weights_gather(): pl.pallas_call(functools.partial(weights_kernel, n), out_shape=[jax.Shape...  27.6 us
    pallas_call x1, Pallas kernels, normalized(): pl.pallas_call(functools.partial(norm_kernel, n, conv.shape[0]), out_shap...  25.7 us
    pallas_call x1, Pallas kernels, gather(): pl.pallas_call(functools.partial(gather_kernel, axis, n, inner), out_shap...  20.5 us
    pallas_call x1, Pallas kernels, reduce(): pl.pallas_call(functools.partial(reduce_kernel, axis, n, parts), out_shap...  17.8 us
    ppermute x2, starting transfers between devices, extended(): lax.ppermute(lax.slice_in_dim(array, length - 1, length, axis=dim), axis,...  9.62 us
    reduce_sum x4, other arithmetic, picked(): jnp.sum(jnp.where(mask, array[None], jnp.zeros((), array.dtype)), axis=1)  4.29 us
    unnamed x49, local copies, waits for them, and re-layouts  4.06 us
  transfers between devices with their start and end apart: 4, of which 0 were waited for; matrix products, arithmetic and copies ran while one was open for 17% of the time, Pallas kernels for 53%

profile of v2, /device:TPU:1, one launch (start us, length us, event | category | flops | bytes accessed | tf_op | source)
XLA Modules:
  0.0 179.8 jit_solution(1944569641428813881)
XLA Ops:
  0.6 1.3 collective-permute-start.1
  1.9 5.6 %collective-permute-start = (bf16[2,6,1,16,256]{4,3,2,1,0:T(8,128)(2,1)}, bf16[2,6,1,16,256]{4,3,2,1,0:T(8,128)(2,1)}, u32[]{:S(2)}, u32[]{:S(2)}) collective-permute-start(bf16[2,6,1,16,256]{4,3,2,1,0:T(8,128)(2,1)} %param.7), channel_id=1, source_target_pairs={{0,1},{1,2},{2,3},{3,4},{4,5},{5,6},{6,7},{7,8},{8,9},{9,10},{10,1... | collective-permute-start | bytes 294920 | tf_op jit(solution)/shard_map/ppermute | solution.py:21
  7.6 0.7 copy.53
  9.4 0.7 multiply_convert_fusion
  12.2 1.3 fusion.49
  13.5 0.7 select_reduce_fusion.4
  15.1 0.8 fusion.46
  16.8 1.3 pad.17.x_ref
  18.1 20.5 %shard_map.110 = bf16[16,8,256]{2,1,0:T(8,128)(2,1)} custom-call(bf16[8,256]{1,0:T(8,128)(2,1)} %pad.17.x_ref), custom_call_target="tpu_custom_call" | custom-call | tf_op jit(solution)/shard_map/pallas_call | solution.py:76
  38.6 0.8 slice_bitcast_fusion.18
  39.7 0.8 copy.63
  40.6 1.0 select_reduce_fusion.3
  41.6 27.6 %shard_map.111 = (bf16[27,32,8,128]{3,2,1,0:T(8,128)(2,1)}, bf16[32,32,128]{2,1,0:T(8,128)(2,1)}) custom-call(bf16[27,8,128]{2,1,0:T(8,128)(2,1)} %bitcast.189, bf16[32,32,128]{2,1,0:T(8,128)(2,1)} %bitcast.180), custom_call_target="tpu_custom_call" | custom-call | tf_op jit(solution)/shard_map/pallas_call | solution.py:208
  69.2 2.8 %fusion.56 = (bf16[9,32,8,128]{3,2,1,0:T(8,128)(2,1)}, bf16[9,32,8,128]{3,2,1,0:T(8,128)(2,1)}, bf16[9,32,8,128]{3,2,1,0:T(8,128)(2,1)}) fusion(bf16[27,32,8,128]{3,2,1,0:T(8,128)(2,1)} %get-tuple-element.13), kind=kLoop, calls=%fused_computation.157 | loop fusion | bytes 3538944 | tf_op jit(solution)/shard_map/slice | solution.py:470
  77.0 0.9 copy.65
  77.9 1.3 fusion.55
  79.4 1.2 fusion.11
  81.2 0.8 copy-done.3
  83.5 1.0 convolution_add_fusion.2
  85.9 25.7 %shard_map.112 = (bf16[2,96,128]{2,1,0:T(8,128)(2,1)}, bf16[2,96,128]{2,1,0:T(8,128)(2,1)}, f32[8,128]{1,0:T(8,128)}) custom-call(f32[2,96,128]{2,1,0:T(8,128)} %bitcast.188, f32[2,96,128]{2,1,0:T(8,128)} %bitcast_convert_fusion.grad_ref, f32[2,96,128]{2,1,0:T(8,128)} %broadcast_in_dim.198.alive_ref, f32[8,128]{1,0:T(8,128)} %broadcast_in_dim.199.count_ref, ...), custom_call_target="tpu_custom_call" | custom-call | tf_op jit(solution)/shard_map/pallas_call | solution.py:378
  111.6 1.4 fusion.2
  114.1 1.3 collective-permute-start.3
  115.4 4.0 %collective-permute-start.2 = (bf16[2,6,1,16,128]{4,3,1,0,2:T(8,128)(2,1)S(1)}, bf16[2,6,1,16,128]{4,3,1,0,2:T(8,128)(2,1)S(1)}, u32[]{:S(2)}, u32[]{:S(2)}) collective-permute-start(bf16[2,6,1,16,128]{4,3,1,0,2:T(8,128)(2,1)S(1)} %bitcast.185), channel_id=1, source_target_pairs={{0,1},{1,2},{2,3},{3,4},{4,5},{5,6},{6,7},{7,8},{8,9},{9,10},{10,1... | collective-permute-start | bytes 147464 | tf_op jit(solution)/shard_map/ppermute | solution.py:21
  119.5 1.1 select_reduce_fusion.y_ref
  120.6 1.4 pad_maximum_fusion
  122.7 30.0 %shard_map.113 = (f32[27,8,128]{2,1,0:T(8,128)}, f32[8,128]{1,0:T(8,128)}, bf16[32,32,128]{2,1,0:T(8,128)(2,1)}) custom-call(bf16[27,16,2,8,128]{4,3,2,1,0:T(8,128)(2,1)} %bitcast.170, f32[8,128]{1,0:T(8,128)} %maximum_maximum_fusion.s_ref, bf16[32,32,128]{2,1,0:T(8,128)(2,1)} %select_reduce_fusion.y_ref), custom_call_target="tpu_custom_call" | custom-call | tf_op jit(solution)/shard_map/pallas_call | solution.py:296
  152.7 1.3 slice_bitcast_fusion.19
  154.0 1.8 %select_reduce_fusion.2 = bf16[4,32,128]{2,1,0:T(8,128)(2,1)} fusion(pred[4,32]{1,0:T(4,128)(4,1)S(1)} %iota_compare_fusion.10, bf16[32,32,128]{2,1,0:T(8,128)(2,1)} %get-tuple-element.18), kind=kLoop, calls=%fused_computation.22 | loop fusion | flops 1032192 | bytes 295040 | tf_op jit(solution)/shard_map/reduce_sum | solution.py:396
  155.8 1.1 copy.66
  157.8 17.8 %shard_map.114 = f32[8,256]{1,0:T(8,128)} custom-call(f32[16,8,256]{2,1,0:T(8,128)} %pad.19.refs_0_), custom_call_target="tpu_custom_call" | custom-call | tf_op jit(solution)/shard_map/pallas_call | solution.py:143
  176.2 0.9 copy-done.4
  178.2 0.9 fusion.8
  (108 shorter events, 17.2 us)
Async XLA Ops:
  0.6 40.0 %copy-start.11 = (bf16[4,2,1,16,128]{4,3,2,1,0:T(8,128)(2,1)S(1)}, bf16[4,2,1,16,128]{4,3,2,1,0:T(8,128)(2,1)}, u32[]{:S(2)}) copy-start(bf16[4,2,1,16,128]{4,3,2,1,0:T(8,128)(2,1)} %param.13) | copy-start | bytes 98308
  0.6 78.8 %collective-permute-start.1 = (bf16[2,6,1,16,256]{4,3,2,1,0:T(8,128)(2,1)}, bf16[2,6,1,16,256]{4,3,2,1,0:T(8,128)(2,1)}, u32[]{:S(2)}, u32[]{:S(2)}) collective-permute-start(bf16[2,6,1,16,256]{4,3,2,1,0:T(8,128)(2,1)} %param.7), channel_id=1, source_target_pairs={{1,0},{2,1},{3,2},{4,3},{5,4},{6,5},{7,6},{8,7},{9,8},{10,9},{11,1... | collective-permute-start | bytes 294920 | tf_op jit(solution)/shard_map/ppermute | solution.py:22
  1.9 77.5 %collective-permute-start = (bf16[2,6,1,16,256]{4,3,2,1,0:T(8,128)(2,1)}, bf16[2,6,1,16,256]{4,3,2,1,0:T(8,128)(2,1)}, u32[]{:S(2)}, u32[]{:S(2)}) collective-permute-start(bf16[2,6,1,16,256]{4,3,2,1,0:T(8,128)(2,1)} %param.7), channel_id=1, source_target_pairs={{0,1},{1,2},{2,3},{3,4},{4,5},{5,6},{6,7},{7,8},{8,9},{9,10},{10,1... | collective-permute-start | bytes 294920 | tf_op jit(solution)/shard_map/ppermute | solution.py:21
  69.2 3.0 %copy-start.15 = (s32[32]{0:T(128)S(1)}, s32[32]{0:T(128)}, u32[]{:S(2)}) copy-start(s32[32]{0:T(128)} %param.9) | copy-start | bytes 388
  69.2 4.0 %copy-start.8 = (bf16[32,32,128]{2,1,0:T(8,128)(2,1)S(1)}, bf16[32,32,128]{2,1,0:T(8,128)(2,1)}, u32[]{:S(2)}) copy-start(bf16[32,32,128]{2,1,0:T(8,128)(2,1)} %get-tuple-element.14) | copy-start | bytes 786436
  69.2 7.8 %copy-start = (bf16[27,32,8,128]{3,2,1,0:T(8,128)(2,1)S(1)}, bf16[27,32,8,128]{3,2,1,0:T(8,128)(2,1)}, u32[]{:S(2)}) copy-start(bf16[27,32,8,128]{3,2,1,0:T(8,128)(2,1)} %get-tuple-element.13) | copy-start | bytes 5308420
  77.9 1.3 copy-start.14
  77.9 1.5 copy-start.9
  81.0 1.1 copy-start.3
  81.2 1.2 copy-start.2
  82.4 1.1 copy-start.1
  111.6 1.4 copy-start.7
  113.0 6.4 %copy-start.13 = (f32[8,128]{1,0:T(8,128)S(1)}, f32[8,128]{1,0:T(8,128)}, u32[]{:S(2)}) copy-start(f32[8,128]{1,0:T(8,128)} %get-tuple-element.16) | copy-start | bytes 12292
  113.0 6.4 %copy-start.10 = (bf16[2,96,128]{2,1,0:T(8,128)(2,1)S(1)}, bf16[2,96,128]{2,1,0:T(8,128)(2,1)}, u32[]{:S(2)}) copy-start(bf16[2,96,128]{2,1,0:T(8,128)(2,1)} %get-tuple-element.17) | copy-start | bytes 147460
  114.1 61.5 %collective-permute-start.3 = (bf16[2,6,1,16,128]{4,3,1,0,2:T(8,128)(2,1)S(1)}, bf16[2,6,1,16,128]{4,3,1,0,2:T(8,128)(2,1)S(1)}, u32[]{:S(2)}, u32[]{:S(2)}) collective-permute-start(bf16[2,6,1,16,128]{4,3,1,0,2:T(8,128)(2,1)S(1)} %bitcast.184), channel_id=1, source_target_pairs={{1,0},{2,1},{3,2},{4,3},{5,4},{6,5},{7,6},{8,7},{9,8},{10,9},{11,1... | collective-permute-start | bytes 147464 | tf_op jit(solution)/shard_map/ppermute | solution.py:22
  115.4 60.2 %collective-permute-start.2 = (bf16[2,6,1,16,128]{4,3,1,0,2:T(8,128)(2,1)S(1)}, bf16[2,6,1,16,128]{4,3,1,0,2:T(8,128)(2,1)S(1)}, u32[]{:S(2)}, u32[]{:S(2)}) collective-permute-start(bf16[2,6,1,16,128]{4,3,1,0,2:T(8,128)(2,1)S(1)} %bitcast.185), channel_id=1, source_target_pairs={{0,1},{1,2},{2,3},{3,4},{4,5},{5,6},{6,7},{7,8},{8,9},{9,10},{10,1... | collective-permute-start | bytes 147464 | tf_op jit(solution)/shard_map/ppermute | solution.py:21
  176.1 1.1 copy-start.4
  176.2 1.3 copy-start.6
  177.1 1.1 copy-start.5
  177.5 1.7 copy-start.12
